TPU v7x, 32 devices: a whole 2x2x4 slice. The times are simulated.
32 devices in a mesh: tm: 16 (over z, y, x), mp: 2 (over core).
Axes of the slice: x: 2, y: 2, z: 4, core: 2. Of those that a mesh axis runs over, the one named last changes fastest.
Arguments:
- filterbank: bfloat16 [4, 16384, 80], P(None, 'tm'), may hold values from -6 to 6
- lengths: int32 [4], replicated, may hold values from 2048 to 4096, as said below
- bank_begin: int32 [4, 1024], P(None, 'tm'), may hold values from 0 to 1023, as said below
- memory_in: bfloat16 [4, 1024, 1024], P(None, 'tm', 'mp'), may hold values from -6 to 6
- w_front: bfloat16 [320, 1024], P(None, 'mp'), may hold values from -0.3125 to 0.3125
- gain_attn: float32 [1024], replicated, may hold values from 0.25 to 1.75
- w_query: bfloat16 [1024, 1024], P(None, 'mp'), may hold values from -0.1875 to 0.1875
- w_key: bfloat16 [1024, 1024], P(None, 'mp'), may hold values from -0.1875 to 0.1875
- w_value: bfloat16 [1024, 1024], P(None, 'mp'), may hold values from -0.1875 to 0.1875
- w_out: bfloat16 [1024, 1024], P('mp'), may hold values from -0.1875 to 0.1875
- gain_ffn: float32 [1024], replicated, may hold values from 0.25 to 1.75
- w_up: bfloat16 [1024, 4096], P(None, 'mp'), may hold values from -0.1875 to 0.1875
- w_down: bfloat16 [4096, 1024], P('mp'), may hold values from -0.09375 to 0.09375
Outputs:
- encoded: bfloat16 [4, 4096, 1024], P(None, 'tm', 'mp')
- memory_out: bfloat16 [4, 1024, 1024], P(None, 'tm', 'mp')
Inputs may be any that keep to these rules, and one draw needn't show every extreme that they name: `lengths`: some utterance has all 4096 frames. For segment i: max(0, i - 32) <= bank_begin <= max(0, i - 16); in each utterance some segment has bank_begin = i - 32.
All inputs are finite; a program needn't handle non-finite values.
Results may differ from a plain program's by a relative error of at most 0.012.
Values may be sent and summed in bfloat16 or wider, within the bound.
A program may use at most 128 MiB of HBM per device.

v0:
```python
import jax
import jax.numpy as jnp
from jax import lax
from jax.sharding import PartitionSpec as P

HEAD_DIM = 64
STACK = 4
SEG = 4
LC = 32
RC = 4
M = 32


epsilon = 1e-05


def from_behind(block, axis, distance):
    devices = range(lax.axis_size(axis))
    route = [(i - distance, i) for i in devices if i - distance in devices]
    return lax.ppermute(block, axis, route)


def normalize(values, gain):
    center = jnp.mean(values, axis=-1, keepdims=True)
    shifted = values - center
    spread = jnp.mean(shifted * shifted, axis=-1, keepdims=True)
    return shifted * lax.rsqrt(spread + epsilon) * gain


def product(inputs, weight):
    flat_rows = inputs.reshape(-1, inputs.shape[-1])
    result = jnp.dot(flat_rows, weight, preferred_element_type=jnp.float32)
    return result.reshape(inputs.shape[:-1] + (weight.shape[1],))


def rounded(values):
    return lax.optimization_barrier(values.astype(jnp.bfloat16)).astype(jnp.float32)


def body(
    filterbank,
    lengths,
    bank_begin,
    memory_in,
    w_front,
    gain_attn,
    w_query,
    w_key,
    w_value,
    w_out,
    gain_ffn,
    w_up,
    w_down,
):
    batch_count = filterbank.shape[0]
    frames_dev = filterbank.shape[1] // STACK
    segs_dev = frames_dev // SEG
    full_width = w_query.shape[0]
    part_width = w_query.shape[1]
    head_count = part_width // HEAD_DIM
    half_width = full_width // lax.axis_size("mp")
    device_index = lax.axis_index("tm")
    model_index = lax.axis_index("mp")
    column_start = model_index * half_width
    first_frame = device_index * frames_dev
    frame_pos = first_frame + jnp.arange(frames_dev, dtype=jnp.int32)
    valid_frame = frame_pos[None, :] < lengths[:, None]
    seg_global = device_index * segs_dev + jnp.arange(segs_dev, dtype=jnp.int32)
    valid_seg = seg_global[None, :] * SEG < lengths[:, None]
    stacked = filterbank.reshape(batch_count, frames_dev, STACK * filterbank.shape[2])
    front_half = jnp.where(valid_frame[:, :, None], product(stacked, w_front), 0.0).astype(
        jnp.bfloat16
    )
    inputs, memory_full = (
        lax.all_gather(front_half, "mp", axis=2, tiled=True),
        lax.all_gather(memory_in, "mp", axis=2, tiled=True),
    )
    inputs_f = inputs.astype(jnp.float32)
    summary = jnp.mean(inputs_f.reshape(batch_count, segs_dev, SEG, full_width), axis=2)
    normed_all = jnp.concatenate(
        [
            normalize(inputs_f, gain_attn),
            normalize(summary, gain_attn),
            normalize(memory_full.astype(jnp.float32), gain_attn),
        ],
        axis=1,
    ).astype(jnp.bfloat16)
    query_rows = product(normed_all[:, : frames_dev + segs_dev], w_query).astype(jnp.bfloat16)
    key_input = jnp.concatenate(
        [normed_all[:, :frames_dev], normed_all[:, frames_dev + segs_dev :]], axis=1
    )
    key_rows = product(key_input, w_key).astype(jnp.bfloat16)
    value_rows = product(key_input, w_value).astype(jnp.bfloat16)
    frame_keys = key_rows[:, :frames_dev]
    frame_values = value_rows[:, :frames_dev]
    bank_pair = jnp.stack([key_rows[:, frames_dev:], value_rows[:, frames_dev:]])
    left_pair = from_behind(
        jnp.stack([frame_keys[:, frames_dev - LC :], frame_values[:, frames_dev - LC :]]), "tm", 1
    )
    right_pair = from_behind(jnp.stack([frame_keys[:, :RC], frame_values[:, :RC]]), "tm", -1)
    hop_count = -(-M // segs_dev)
    gathered = []
    moving = bank_pair
    moving = from_behind(moving, "tm", 1)
    gathered.insert(0, moving)
    bank_all = jnp.concatenate(gathered + [bank_pair], axis=2)
    all_keys = jnp.concatenate([left_pair[0], frame_keys, right_pair[0], bank_all[0]], axis=1)
    all_values = jnp.concatenate([left_pair[1], frame_values, right_pair[1], bank_all[1]], axis=1)
    query_count = frames_dev + segs_dev
    local_seg = jnp.concatenate(
        [jnp.arange(frames_dev, dtype=jnp.int32) // SEG, jnp.arange(segs_dev, dtype=jnp.int32)]
    )
    query_seg = device_index * segs_dev + local_seg
    bank_floor = jnp.concatenate([jnp.repeat(bank_begin, SEG, axis=1), bank_begin], axis=1)
    key_pos = first_frame - LC + jnp.arange(LC + frames_dev + RC, dtype=jnp.int32)
    key_grid = key_pos[None, None, :]
    seg_grid = query_seg[None, :, None]
    frame_allowed = (
        (key_grid >= seg_grid * SEG - LC)
        & (key_grid < (seg_grid + 1) * SEG + RC)
        & (key_grid >= 0)
        & (key_grid < lengths[:, None, None])
    )
    bank_seg = (device_index - hop_count) * segs_dev + jnp.arange(
        (hop_count + 1) * segs_dev, dtype=jnp.int32
    )
    bank_grid = bank_seg[None, None, :]
    bank_allowed = (bank_grid >= bank_floor[:, :, None]) & (bank_grid <= seg_grid - 1)
    allowed = jnp.concatenate([frame_allowed, bank_allowed], axis=2)
    query_heads = query_rows.reshape(batch_count, query_count, head_count, HEAD_DIM)
    key_heads = all_keys.reshape(batch_count, -1, head_count, HEAD_DIM)
    value_heads = all_values.reshape(batch_count, -1, head_count, HEAD_DIM)
    scores = jnp.einsum(
        "bqhd,bkhd->bhqk", query_heads, key_heads, preferred_element_type=jnp.float32
    ) * HEAD_DIM ** (-0.5)
    weights = jnp.where(allowed[:, None], jnp.exp(scores), 0.0)
    shares = (weights / jnp.sum(weights, axis=-1, keepdims=True)).astype(jnp.bfloat16)
    context = jnp.einsum("bhqk,bkhd->bqhd", shares, value_heads, preferred_element_type=jnp.float32)
    context = context.astype(jnp.bfloat16).reshape(batch_count, query_count, part_width)
    mixed_term = rounded(product(context, w_out))
    frame_term = mixed_term[:, :frames_dev]
    summary_term = mixed_term[:, frames_dev:]
    attention, memory_half = (
        lax.psum_scatter(
            frame_term.astype(jnp.bfloat16), "mp", scatter_dimension=2, tiled=True
        ).astype(jnp.float32),
        lax.psum_scatter(
            summary_term.astype(jnp.bfloat16), "mp", scatter_dimension=2, tiled=True
        ).astype(jnp.float32),
    )
    residual = (front_half.astype(jnp.float32) + attention).astype(jnp.bfloat16)
    residual_f = residual.astype(jnp.float32)
    first_moment, second_moment = lax.psum(
        (jnp.sum(residual_f, axis=-1), jnp.sum(residual_f * residual_f, axis=-1)), "mp"
    )
    center = first_moment / full_width
    spread = second_moment / full_width - center * center
    gain_half = lax.dynamic_slice_in_dim(gain_ffn, column_start, half_width, 0)
    normed_half = (
        (residual_f - center[..., None]) * lax.rsqrt(spread[..., None] + epsilon) * gain_half
    ).astype(jnp.bfloat16)
    normed_ffn = lax.all_gather(normed_half, "mp", axis=2, tiled=True)
    hidden = jax.nn.gelu(product(normed_ffn, w_up)).astype(jnp.bfloat16)
    feed_half = lax.psum_scatter(
        rounded(product(hidden, w_down)).astype(jnp.bfloat16), "mp", scatter_dimension=2, tiled=True
    ).astype(jnp.float32)
    encoded = jnp.where(
        valid_frame[:, :, None], residual.astype(jnp.float32) + feed_half, 0.0
    ).astype(jnp.bfloat16)
    memory_out = jnp.where(valid_seg[:, :, None], memory_half, 0.0).astype(jnp.bfloat16)
    return (encoded, memory_out)


def solution(mesh):
    in_specs = (
        P(None, "tm", None),
        P(),
        P(None, "tm"),
        P(None, "tm", "mp"),
        P(None, "mp"),
        P(),
        P(None, "mp"),
        P(None, "mp"),
        P(None, "mp"),
        P("mp", None),
        P(),
        P(None, "mp"),
        P("mp", None),
    )
    out_specs = (P(None, "tm", "mp"), P(None, "tm", "mp"))
    return jax.shard_map(body, mesh=mesh, in_specs=in_specs, out_specs=out_specs, check_vma=False)
```

profile of v0, /device:TPU:0, one launch (start us, length us, event | category | flops | bytes accessed | tf_op | source)
XLA Modules:
  0.0 166.0 jit_solution(9979901539850414377)
XLA Ops:
  7.3 1.6 copy.25
  8.9 0.7 dot_general.31
  9.6 0.1 broadcast_compare_fusion.2
  9.7 2.6 %select_convert_fusion = bf16[4,256,512]{2,1,0:T(8,128)(2,1)} fusion(bf16[4,256,320]{2,1,0:T(8,128)(2,1)S(1)} %dot_general.31, pred[4,256]{1,0:T(4,128)(4,1)S(1)} %broadcast_compare_fusion.2, bf16[320,512]{1,0:T(8,128)(2,1)} %param.17), kind=kOutput, calls=%fused_computation.55 | convolution fusion | flops 336592896 | bytes 2032640 | tf_op jit(solution)/shard_map/dot_general | solution.py:32
  12.4 2.3 %all_gather.10 = bf16[4,64,1024]{2,1,0:T(8,128)(2,1)S(1)} all-gather(bf16[4,64,512]{2,1,0:T(8,128)(2,1)S(1)} %copy-done.18), channel_id=1, replica_groups=mesh['tm'=16,'mp'=2] {'mp'}, dimensions={2}, use_global_device_ids=true | all-gather | bytes 786432 | tf_op jit(solution)/shard_map/all_gather | solution.py:76
  14.7 0.1 broadcast_in_dim.40
  14.8 0.1 reshape.351
  15.0 0.1 convert_reduce_fusion.2
  15.2 0.1 broadcast_compare_fusion.1
  15.2 0.1 broadcast_compare_fusion
  15.3 0.2 and_and_fusion
  15.5 0.2 compare_and_fusion
  15.7 0.3 broadcast_and_fusion
  16.0 1.1 pad_add_fusion
  17.2 0.3 fusion.66
  17.5 8.4 %all-gather.3.cloned.1.call-done = bf16[4,256,1024]{2,1,0:T(8,128)(2,1)} async-done(((bf16[4,256,512]{2,1,0:T(8,128)(2,1)}), bf16[4,256,1024]{2,1,0:T(8,128)(2,1)}) %all-gather.3.cloned.1.call-update) | async-done | bytes 2097168 | tf_op jit(solution)/shard_map/all_gather | solution.py:75
  25.8 4.8 %reshape.352 = f32[4,64,4,1024]{3,2,1,0:T(4,128)} reshape(bf16[4,256,1024]{2,1,0:T(8,128)(2,1)} %all-gather.3.cloned.1.call-done) | data formatting | bytes 6291456 | tf_op jit(solution)/shard_map/reshape | solution.py:79
  30.6 5.9 %reduce_sum.94 = f32[4,64,1024]{2,1,0:T(8,128)} reduce(f32[4,64,4,1024]{3,2,1,0:T(4,128)} %reshape.352, f32[]{:T(128)} %constant.29.clone.1), dimensions={2}, to_apply=%region_4.5 | reduce | flops 786432 | bytes 5242884 | tf_op jit(solution)/shard_map/reduce_sum | solution.py:79
  36.5 1.4 multiply_reduce_fusion.2
  37.9 1.6 multiply_reduce_fusion.1
  39.5 0.3 convert_reduce_fusion.1
  39.9 0.7 multiply_reduce_fusion
  40.6 0.4 fusion.68
  41.0 0.7 multiply_convert_fusion
  41.7 0.5 copy-done.23
  42.2 1.5 fusion.59
  43.8 1.5 fusion.60
  45.5 0.8 pad_maximum_fusion.8
  46.3 4.5 %collective-permute-start = (bf16[2,4,32,512]{3,2,1,0:T(8,128)(2,1)}, bf16[2,4,32,512]{3,2,1,0:T(8,128)(2,1)}, u32[]{:S(2)}, u32[]{:S(2)}) collective-permute-start(bf16[2,4,32,512]{3,2,1,0:T(8,128)(2,1)} %pad_maximum_fusion.8), channel_id=1, source_target_pairs={{0,2},{2,4},{4,6},{6,8},{8,10},{10,12},{12,14},{14,16},{16,18},{18... | collective-permute-start | bytes 786440 | tf_op jit(solution)/shard_map/ppermute | solution.py:20
  50.8 1.3 collective-permute-start.1
  52.1 0.9 pad_maximum_fusion.7
  52.9 5.3 %collective-permute-start.2 = (bf16[2,4,64,512]{3,2,1,0:T(8,128)(2,1)}, bf16[2,4,64,512]{3,2,1,0:T(8,128)(2,1)}, u32[]{:S(2)}, u32[]{:S(2)}) collective-permute-start(bf16[2,4,64,512]{3,2,1,0:T(8,128)(2,1)} %pad_maximum_fusion.7), channel_id=1, source_target_pairs={{0,2},{2,4},{4,6},{6,8},{8,10},{10,12},{12,14},{14,16},{16,18},{18... | collective-permute-start | bytes 1572872 | tf_op jit(solution)/shard_map/ppermute | solution.py:20
  58.3 2.6 %fusion.61 = bf16[4,320,512]{2,1,0:T(8,128)(2,1)} fusion(bf16[4,64,1024]{2,1,0:T(8,128)(2,1)S(1)} %get-tuple-element.16, bf16[4,256,1024]{2,1,0:T(8,128)(2,1)S(1)} %multiply_convert_fusion, bf16[1024,512]{1,0:T(8,128)(2,1)S(1)} %copy-done.25), kind=kOutput, calls=%fused_computation.63 | convolution fusion | flops 1348075520 | bytes 4980736 | tf_op jit(solution)/shard_map/dot_general | solution.py:32
  60.9 1.2 slice-done.1
  62.1 1.3 copy.32
  63.4 2.6 %copy.31 = bf16[4,320,512]{1,2,0:T(8,128)(2,1)} copy(bf16[4,320,512]{2,1,0:T(8,128)(2,1)} %fusion.61) | data formatting | bytes 2621440 | tf_op jit(solution)/shard_map/convert_element_type | solution.py:88
  66.0 1.3 copy.27
  67.4 1.1 copy.42
  68.5 1.1 copy.40
  69.5 1.0 fusion.86
  70.5 1.0 copy.41
  71.5 1.1 copy.39
  72.6 1.1 maximum_maximum_fusion
  73.7 0.1 fusion.85
  73.8 1.0 copy.33
  74.8 0.3 copy.28
  75.2 12.9 %fusion = (f32[4,8,320]{2,1,0:T(8,128)S(1)}, f32[4,8,320,420]{2,3,1,0:T(8,128)}) fusion(pred[4,320,420]{1,2,0:T(8,128)(4,1)} %pad_add_fusion, bf16[4,320,8,64]{1,3,2,0:T(8,128)(2,1)} %bitcast.57, bf16[4,128,8,64]{1,3,2,0:T(8,128)(2,1)} %bitcast.65, bf16[4,4,8,64]{1,3,2,0:T(8,128)(2,1)} %bitcast.63, bf16[4,256,8,64]{1,3,2,0:T(8,128)(2,1)S(1)} %bitcast.59, ...), kind=kOutput, calls=%fused_computation.2 | convolution fusion | flops 570275840 | bytes 20812800 | tf_op jit(solution)/shard_map/bqhd,bkhd->bhqk/dot_general | solution.py:133
  88.1 10.9 %fusion.54 = bf16[4,8,64,320]{3,2,1,0:T(8,128)(2,1)S(1)} fusion(f32[4,8,320,420]{2,3,1,0:T(8,128)} %get-tuple-element.21, f32[4,8,320]{2,1,0:T(8,128)S(1)} %get-tuple-element.20, pred[4,320,420]{1,2,0:T(8,128)(4,1)S(1)} %copy-done.15, bf16[4,128,8,64]{1,3,2,0:T(8,128)(2,1)S(1)} %bitcast.64, bf16[4,4,8,64]{1,3,2,0:T(8,128)(2,1)S(1)} %bitcast.62, ...), kind=kOutput, calls=%fused_computation.58 | convolution fusion | flops 575242240 | bytes 20812800 | tf_op jit(solution)/shard_map/bhqk,bkhd->bqhd/dot_general | solution.py:138
  99.1 1.6 convolution_convert_fusion
  100.7 1.5 copy-done.8
  102.2 1.5 slice.94
  103.7 0.3 all-gather.5.cloned.1.call-start
  104.0 0.1 dynamic_slice.3
  104.0 9.9 %reduce-scatter.4.cloned.1.call-done = bf16[4,256,512]{2,1,0:T(8,128)(2,1)} async-done(((bf16[4,256,1024]{2,1,0:T(8,128)(2,1)}), bf16[4,256,512]{2,1,0:T(8,128)(2,1)}) %reduce-scatter.4.cloned.1.call-update) | async-done | bytes 1048592 | tf_op jit(solution)/shard_map/reduce_scatter | solution.py:144
  113.9 1.8 %convert_reduce_fusion = (f32[4,256]{1,0:T(4,128)S(1)}, f32[4,256]{1,0:T(4,128)S(1)}, bf16[4,256,512]{2,1,0:T(8,128)(2,1)S(1)}) fusion(bf16[4,256,512]{2,1,0:T(8,128)(2,1)} %reduce-scatter.4.cloned.1.call-done, bf16[4,256,512]{2,1,0:T(8,128)(2,1)S(1)} %copy-done.5), kind=kLoop, calls=%fused_computation.25 | loop fusion | flops 4192256 | bytes 3153920 | tf_op jit(solution)/shard_map/reduce_sum | solution.py:154
  115.7 2.5 %all-reduce = (f32[4,256]{1,0:T(4,128)S(1)}, f32[4,256]{1,0:T(4,128)S(1)}) all-reduce(f32[4,256]{1,0:T(4,128)S(1)} %get-tuple-element.3, f32[4,256]{1,0:T(4,128)S(1)} %get-tuple-element.2), channel_id=1, replica_groups=mesh['tm'=16,'mp'=2] {'mp'}, use_global_device_ids=true, to_apply=%region_12.13 | all-reduce | flops 2048 | bytes 16384 | tf_op jit(solution)/shard_map/psum | solution.py:153
  118.2 1.4 fusion.28
  119.7 1.9 %slice.95 = bf16[4,64,1024]{2,1,0:T(8,128)(2,1)} slice(bf16[4,320,1024]{2,1,0:T(8,128)(2,1)} %copy-done.8), slice={[0:4], [256:320], [0:1024]} | slice | bytes 1048576 | tf_op jit(solution)/shard_map/slice | solution.py:142
  121.6 10.0 %all-gather.5.cloned.1.call-done = bf16[4,256,1024]{2,1,0:T(8,128)(2,1)} async-done(((bf16[4,256,512]{2,1,0:T(8,128)(2,1)}), bf16[4,256,1024]{2,1,0:T(8,128)(2,1)}) %all-gather.5.cloned.1.call-update) | async-done | bytes 2097168 | tf_op jit(solution)/shard_map/all_gather | solution.py:162
  131.6 14.3 %fusion.47 = bf16[4,256,1024]{2,1,0:T(8,128)(2,1)} fusion(bf16[2048,1024]{1,0:T(8,128)(2,1)} %param.25, bf16[4,256,1024]{2,1,0:T(8,128)(2,1)} %all-gather.5.cloned.1.call-done, bf16[1024,2048]{1,0:T(8,128)(2,1)} %param.24), kind=kOutput, calls=%fused_computation.57 | convolution fusion | flops 8609857536 | bytes 12582912 | tf_op jit(solution)/shard_map/dot_general | solution.py:32
  146.0 0.1 broadcast_compare_fusion.3
  146.1 1.8 %select_convert_fusion.1 = bf16[4,64,512]{2,1,0:T(8,128)(2,1)} fusion(bf16[4,64,512]{2,1,0:T(8,128)(2,1)} %reduce-scatter.8.cloned.1.call-done, pred[4,64]{1,0:T(4,128)(4,1)S(1)} %broadcast_compare_fusion.3), kind=kLoop, calls=%fused_computation.82 | loop fusion | flops 393216 | bytes 524544 | tf_op jit(solution)/shard_map/convert_element_type | solution.py:170
  147.8 9.1 %reduce-scatter.6.cloned.1.call-done = bf16[4,256,512]{2,1,0:T(8,128)(2,1)} async-done(((bf16[4,256,1024]{2,1,0:T(8,128)(2,1)}), bf16[4,256,512]{2,1,0:T(8,128)(2,1)}) %reduce-scatter.6.cloned.1.call-update) | async-done | bytes 1048592 | tf_op jit(solution)/shard_map/reduce_scatter | solution.py:164
  156.9 2.5 %fusion.31 = bf16[4,256,512]{2,1,0:T(8,128)(2,1)} fusion(bf16[4,256,512]{2,1,0:T(8,128)(2,1)S(1)} %get-tuple-element.6, bf16[4,256,512]{2,1,0:T(8,128)(2,1)} %reduce-scatter.6.cloned.1.call-done, pred[4,256]{1,0:T(4,128)(4,1)S(1)} %broadcast_compare_fusion.2), kind=kLoop, calls=%fused_computation.38 | loop fusion | flops 2621440 | bytes 3146752 | tf_op jit(solution)/shard_map/convert_element_type | solution.py:169
  (87 shorter events, 0.6 us)
Async XLA Ops:
  7.2 91.9 %copy-start = (bf16[512,1024]{1,0:T(8,128)(2,1)S(1)}, bf16[512,1024]{1,0:T(8,128)(2,1)}, u32[]{:S(2)}) copy-start(bf16[512,1024]{1,0:T(8,128)(2,1)} %param.22) | copy-start | bytes 3145732
  7.2 2.4 %copy-start.21 = (s32[4]{0:T(128)S(1)}, s32[4]{0:T(128)}, u32[]{:S(2)}) copy-start(s32[4]{0:T(128)} %param.14) | copy-start | bytes 52
  7.2 18.6 %all-gather.3.cloned.1.call-start = ((), (), s32[]{:S(2)}) async-start(), calls=%async_computation.3 | async-start | bytes 3145728 | tf_op jit(solution)/shard_map/all_gather | solution.py:75
  8.9 3.5 %copy-start.18 = (bf16[4,64,512]{2,1,0:T(8,128)(2,1)S(1)}, bf16[4,64,512]{2,1,0:T(8,128)(2,1)}, u32[]{:S(2)}) copy-start(bf16[4,64,512]{2,1,0:T(8,128)(2,1)} %param.16) | copy-start | bytes 786436
  9.6 5.2 %copy-start.20 = (s32[4,64]{1,0:T(4,128)S(1)}, s32[4,64]{1,0:T(4,128)}, u32[]{:S(2)}) copy-start(s32[4,64]{1,0:T(4,128)} %param.15) | copy-start | bytes 3076
  12.3 101.6 %reduce-scatter.4.cloned.1.call-start = ((), (), s32[]{:S(2)}) async-start(), calls=%async_computation.4 | async-start | bytes 3145728 | tf_op jit(solution)/shard_map/reduce_scatter | solution.py:144
  14.7 11.1 %copy-start.3 = (bf16[4,64,1024]{2,1,0:T(8,128)(2,1)}, bf16[4,64,1024]{2,1,0:T(8,128)(2,1)S(1)}, u32[]{:S(2)}) copy-start(bf16[4,64,1024]{2,1,0:T(8,128)(2,1)S(1)} %all_gather.10) | copy-start | bytes 1572868
  30.6 9.0 %copy-start.1 = (bf16[4,256,1024]{2,1,0:T(8,128)(2,1)S(1)}, bf16[4,256,1024]{2,1,0:T(8,128)(2,1)}, u32[]{:S(2)}) copy-start(bf16[4,256,1024]{2,1,0:T(8,128)(2,1)} %all-gather.3.cloned.1.call-done) | copy-start | bytes 6291460
  37.9 2.7 %copy-start.2 = (f32[4,64,1024]{2,1,0:T(8,128)S(1)}, f32[4,64,1024]{2,1,0:T(8,128)}, u32[]{:S(2)}) copy-start(f32[4,64,1024]{2,1,0:T(8,128)} %reduce_sum.94) | copy-start | bytes 3145732
  37.9 2.7 %copy-start.4 = (bf16[4,64,1024]{2,1,0:T(8,128)(2,1)S(1)}, bf16[4,64,1024]{2,1,0:T(8,128)(2,1)}, u32[]{:S(2)}) copy-start(bf16[4,64,1024]{2,1,0:T(8,128)(2,1)} %copy-done.3) | copy-start | bytes 1572868
  37.9 2.7 %copy-start.19 = (f32[1024]{0:T(1024)S(1)}, f32[1024]{0:T(1024)}, u32[]{:S(2)}) copy-start(f32[1024]{0:T(1024)} %param.18) | copy-start | bytes 12292
  41.0 1.2 copy-start.23
  42.2 1.5 copy-start.24
  43.8 17.1 %copy-start.7 = (bf16[4,320,512]{2,1,0:T(8,128)(2,1)}, bf16[4,320,512]{2,1,0:T(8,128)(2,1)S(1)}, u32[]{:S(2)}) copy-start(bf16[4,320,512]{2,1,0:T(8,128)(2,1)S(1)} %fusion.59) | copy-start | bytes 3932164
  45.4 15.6 %copy-start.6 = (bf16[4,320,512]{2,1,0:T(8,128)(2,1)}, bf16[4,320,512]{2,1,0:T(8,128)(2,1)S(1)}, u32[]{:S(2)}) copy-start(bf16[4,320,512]{2,1,0:T(8,128)(2,1)S(1)} %fusion.60) | copy-start | bytes 3932164
  45.4 12.9 %copy-start.25 = (bf16[1024,512]{1,0:T(8,128)(2,1)S(1)}, bf16[1024,512]{1,0:T(8,128)(2,1)}, u32[]{:S(2)}) copy-start(bf16[1024,512]{1,0:T(8,128)(2,1)} %param.19) | copy-start | bytes 3145732
  45.5 6.6 %copy-start.9 = (bf16[1,4,64,512]{3,2,1,0:T(8,128)(2,1)}, bf16[1,4,64,512]{3,2,1,0:T(8,128)(2,1)S(1)}, u32[]{:S(2)}) copy-start(bf16[1,4,64,512]{3,2,1,0:T(8,128)(2,1)S(1)} %get-tuple-element.22) | copy-start | bytes 786436
  45.5 7.5 %copy-start.11 = (bf16[1,4,64,512]{3,2,1,0:T(8,128)(2,1)}, bf16[1,4,64,512]{3,2,1,0:T(8,128)(2,1)S(1)}, u32[]{:S(2)}) copy-start(bf16[1,4,64,512]{3,2,1,0:T(8,128)(2,1)S(1)} %get-tuple-element.23) | copy-start | bytes 786436
  46.3 23.3 %collective-permute-start = (bf16[2,4,32,512]{3,2,1,0:T(8,128)(2,1)}, bf16[2,4,32,512]{3,2,1,0:T(8,128)(2,1)}, u32[]{:S(2)}, u32[]{:S(2)}) collective-permute-start(bf16[2,4,32,512]{3,2,1,0:T(8,128)(2,1)} %pad_maximum_fusion.8), channel_id=1, source_target_pairs={{0,2},{2,4},{4,6},{6,8},{8,10},{10,12},{12,14},{14,16},{16,18},{18... | collective-permute-start | bytes 786440 | tf_op jit(solution)/shard_map/ppermute | solution.py:20
  50.8 16.6 %collective-permute-start.1 = (bf16[2,4,4,512]{3,2,1,0:T(4,128)(2,1)S(1)}, bf16[2,4,4,512]{3,2,1,0:T(4,128)(2,1)S(1)}, u32[]{:S(2)}, u32[]{:S(2)}) collective-permute-start(bf16[2,4,4,512]{3,2,1,0:T(4,128)(2,1)S(1)} %pad_maximum_fusion.9), channel_id=1, source_target_pairs={{2,0},{4,2},{6,4},{8,6},{10,8},{12,10},{14,12},{16,14},{18,16},{20... | collective-permute-start | bytes 98312 | tf_op jit(solution)/shard_map/ppermute | solution.py:20
  52.9 19.7 %collective-permute-start.2 = (bf16[2,4,64,512]{3,2,1,0:T(8,128)(2,1)}, bf16[2,4,64,512]{3,2,1,0:T(8,128)(2,1)}, u32[]{:S(2)}, u32[]{:S(2)}) collective-permute-start(bf16[2,4,64,512]{3,2,1,0:T(8,128)(2,1)} %pad_maximum_fusion.7), channel_id=1, source_target_pairs={{0,2},{2,4},{4,6},{6,8},{8,10},{10,12},{12,14},{14,16},{16,18},{18... | collective-permute-start | bytes 1572872 | tf_op jit(solution)/shard_map/ppermute | solution.py:20
  60.9 1.2 slice-start.1
  62.1 3.9 %slice-start = ((bf16[4,320,512]{2,1,0:T(8,128)(2,1)}), bf16[4,256,512]{2,1,0:T(8,128)(2,1)S(1)}, s32[]{:S(2)}) async-start(bf16[4,320,512]{2,1,0:T(8,128)(2,1)} %copy-done.6), calls=%async_computation.8 | async-start | bytes 2097152 | tf_op jit(solution)/shard_map/slice | solution.py:95
  66.0 6.6 %copy-start.10 = (bf16[1,4,64,512]{3,2,1,0:T(8,128)(2,1)S(1)}, bf16[1,4,64,512]{3,2,1,0:T(8,128)(2,1)}, u32[]{:S(2)}) copy-start(bf16[1,4,64,512]{3,2,1,0:T(8,128)(2,1)} %copy-done.9) | copy-start | bytes 786436
  66.0 6.6 %copy-start.12 = (bf16[1,4,64,512]{3,2,1,0:T(8,128)(2,1)S(1)}, bf16[1,4,64,512]{3,2,1,0:T(8,128)(2,1)}, u32[]{:S(2)}) copy-start(bf16[1,4,64,512]{3,2,1,0:T(8,128)(2,1)} %copy-done.11) | copy-start | bytes 786436
  73.7 1.4 copy-start.14
  75.1 13.0 %copy-start.13 = (bf16[4,256,512]{1,2,0:T(8,128)(2,1)S(1)}, bf16[4,256,512]{1,2,0:T(8,128)(2,1)}, u32[]{:S(2)}) copy-start(bf16[4,256,512]{1,2,0:T(8,128)(2,1)} %copy.27) | copy-start | bytes 3145732
  75.1 13.0 %copy-start.15 = (pred[4,320,420]{1,2,0:T(8,128)(4,1)S(1)}, pred[4,320,420]{1,2,0:T(8,128)(4,1)}, u32[]{:S(2)}) copy-start(pred[4,320,420]{1,2,0:T(8,128)(4,1)} %pad_add_fusion) | copy-start | bytes 1612804
  75.1 13.0 %copy-start.16 = (bf16[1,4,32,512]{2,3,1,0:T(8,128)(2,1)S(1)}, bf16[1,4,32,512]{2,3,1,0:T(8,128)(2,1)}, u32[]{:S(2)}) copy-start(bf16[1,4,32,512]{2,3,1,0:T(8,128)(2,1)} %copy.39) | copy-start | bytes 393220
  75.1 13.0 %copy-start.17 = (bf16[1,4,4,512]{2,3,1,0:T(8,128)(2,1)S(1)}, bf16[1,4,4,512]{2,3,1,0:T(8,128)(2,1)}, u32[]{:S(2)}) copy-start(bf16[1,4,4,512]{2,3,1,0:T(8,128)(2,1)} %copy.40) | copy-start | bytes 49156
  100.7 1.5 copy-start.8
  102.2 1.8 %copy-start.22 = (f32[1024]{0:T(1024)S(1)}, f32[1024]{0:T(1024)}, u32[]{:S(2)}) copy-start(f32[1024]{0:T(1024)} %param.23) | copy-start | bytes 12292
  102.2 11.8 %copy-start.5 = (bf16[4,256,512]{2,1,0:T(8,128)(2,1)S(1)}, bf16[4,256,512]{2,1,0:T(8,128)(2,1)}, u32[]{:S(2)}) copy-start(bf16[4,256,512]{2,1,0:T(8,128)(2,1)} %select_convert_fusion) | copy-start | bytes 3145732
  103.7 27.9 %all-gather.5.cloned.1.call-start = ((), (), s32[]{:S(2)}) async-start(), calls=%async_computation.5 | async-start | bytes 3145728 | tf_op jit(solution)/shard_map/all_gather | solution.py:162
  119.6 26.4 %reduce-scatter.8.cloned.1.call-start = ((), (), s32[]{:S(2)}) async-start(), calls=%async_computation.7 | async-start | bytes 786432 | tf_op jit(solution)/shard_map/reduce_scatter | solution.py:147
  121.6 35.3 %reduce-scatter.6.cloned.1.call-start = ((), (), s32[]{:S(2)}) async-start(), calls=%async_computation.6 | async-start | bytes 3145728 | tf_op jit(solution)/shard_map/reduce_scatter | solution.py:164
Sparse Core Ops, SparseCore 0:
  12.5 13.2 all-gather.2
  103.8 10.0 reduce-scatter.3
  119.7 11.8 all-gather.4
  133.7 9.0 reduce-scatter.7
  146.1 10.7 reduce-scatter.5
where the time goes:
time: 167 us; the launch traced here: 166 us
  matrix products  48.1 us (29%)
  waiting for transfers between devices  37.4 us (22%)
  local copies, waits for them, and re-layouts  26 us (16%)
  other arithmetic  23.9 us (14%)
  between operations  14.3 us (9%)
  starting transfers between devices  11.5 us (7%)
  blocking collectives  4.79 us (3%)
    dot_general x6, matrix products, product(): result = jnp.dot(flat_rows, weight, preferred_element_type=jnp.float32)  24.3 us
    dot_general x1, matrix products, body(): jnp.einsum('bqhd,bkhd->bhqk', query_heads, key_heads, preferred_element_t...  12.9 us
    ppermute x3, starting transfers between devices, from_behind(): return lax.ppermute(block, axis, route)  11.1 us
    dot_general x1, matrix products, body(): jnp.einsum('bhqk,bkhd->bqhd', shares, value_heads, preferred_element_type...  10.9 us
    all_gather x1, waiting for transfers between devices, body(): normed_ffn = lax.all_gather(normed_half, 'mp', axis=2, tiled=True)  9.98 us
    reduce_scatter x1, waiting for transfers between devices, body(): lax.psum_scatter(frame_term.astype(jnp.bfloat16), 'mp', scatter_dimension...  9.89 us
    reduce_scatter x1, waiting for transfers between devices, body(): lax.psum_scatter(rounded(product(hidden, w_down)).astype(jnp.bfloat16), '...  9.09 us
    all_gather x1, waiting for transfers between devices, body(): lax.all_gather(front_half, 'mp', axis=2, tiled=True)  8.35 us
  transfers between devices with their start and end apart: 8, of which 4 were waited for; matrix products, arithmetic and copies ran while one was open for 21% of the time, Pallas kernels for 0%

commit v1 on v0

v1 whole, which is shorter than its diff:
```python
import functools
import math

import jax
import jax.numpy as jnp
from jax import lax
from jax.experimental import pallas as pl
from jax.experimental.pallas import tpu as pltpu
from jax.sharding import PartitionSpec as P

HEAD_DIM = 64
STACK = 4
SEG = 4
LC = 32
RC = 4
M = 32

TQ = 128
TS = TQ // SEG
TR = TQ + TS
KB = TS + M
KF = 256 - KB
RB = 16
CH = 32

EPS = 1e-05
NEG = -1e30
F32 = jnp.float32
BF16 = jnp.bfloat16
MESH = pl.DeviceIdType.MESH


def dot(a, b):
    return jnp.dot(a, b, preferred_element_type=F32)


def normed_rows(x, gain):
    width = x.shape[-1]
    center = jnp.sum(x, axis=-1, keepdims=True) * (1.0 / width)
    shifted = x - center
    spread = jnp.sum(shifted * shifted, axis=-1, keepdims=True) * (1.0 / width)
    return (shifted * lax.rsqrt(spread + EPS) * gain).astype(BF16)


def gelu(v):
    inner = math.sqrt(2.0 / math.pi) * (v + 0.044715 * (v * v * v))
    return 0.5 * v * (1.0 + jnp.tanh(inner))


def kernel(
    n_tm,
    lengths, bank, gain_a, gain_f, fb_h, mem_h, wf_h, wq_h, wk_h, wv_h, wo_h, wu_h, wd_h,
    enc_h, mo_h,
    fbv, fb32, fbl, fbr, wf, mem, memh, wq, wk, wv, wo, wu, wd,
    inp, nrm, qt, kf, vf, kb, vb, bias, ctx, part, precv, sums, srecv,
    hid, act, feed, frecv, outb, moutb,
    lsem, osem, ssem, rsem, psend, prsem, msend, mrsem, fsend, frsem,
):
    utts, raw, ch = fb_h.shape
    fd = raw // STACK
    sd = fd // SEG
    half = mem_h.shape[2]
    full = 2 * half
    ff = wu_h.shape[1]
    tiles = fd // TQ
    me = lax.axis_index("tm")
    mp = lax.axis_index("mp")
    other = 1 - mp
    nxt = lax.rem(me + 1, n_tm)
    prv = lax.rem(me + n_tm - 1, n_tm)
    partner_id = (me, other)
    next_id = (nxt, mp)
    prev_id = (prv, mp)
    first = me * fd
    seg0 = me * sd

    barrier = pltpu.get_barrier_semaphore()
    for target in (partner_id, next_id, prev_id):
        pl.semaphore_signal(barrier, inc=1, device_id=target, device_id_type=MESH)

    def local(i, src, dst):
        return pltpu.make_async_copy(src, dst, lsem.at[i])

    c_wf = local(0, wf_h, wf.at[mp])
    c_fb = local(1, fb_h, fbv)
    c_mem = local(2, mem_h, mem.at[mp])
    c_q = local(3, wq_h, wq)
    c_k = local(4, wk_h, wk)
    c_v = local(5, wv_h, wv)
    c_o = [local(6 + g, wo_h.at[:, pl.ds(g * half, half)], wo.at[g]) for g in range(2)]
    c_u = local(8, wu_h, wu)
    c_d = [local(9 + g, wd_h.at[:, pl.ds(g * half, half)], wd.at[g]) for g in range(2)]
    for c in (c_wf, c_fb, c_mem, c_q, c_k, c_v, *c_o, c_u, *c_d):
        c.start()

    def remote(i, src, dst, target, send=ssem, recv=rsem):
        return pltpu.make_async_remote_copy(
            src_ref=src, dst_ref=dst, send_sem=send.at[i], recv_sem=recv.at[i],
            device_id=target, device_id_type=MESH,
        )

    pl.semaphore_wait(barrier, 3)
    r_wf = remote(0, wf_h, wf.at[mp], partner_id)
    r_mem = remote(1, mem_h, mem.at[mp], partner_id)
    r_fbl = remote(2, fb_h.at[:, pl.ds(raw - STACK * LC, STACK * LC), :], fbl, next_id)
    r_memh = remote(3, mem_h.at[:, pl.ds(sd - M, M), :], memh.at[mp], next_id)
    r_fbr = remote(4, fb_h.at[:, pl.ds(0, STACK * RC), :], fbr, prev_id)
    r_fwd = remote(5, memh.at[mp], memh.at[mp], partner_id)
    for r in (r_wf, r_mem, r_fbl, r_memh, r_fbr):
        r.start()
    a_wf = remote(0, wf_h, wf.at[other], partner_id)
    a_mem = remote(1, mem_h, mem.at[other], partner_id)
    a_fwd = remote(5, memh.at[mp], memh.at[other], partner_id)

    avg = jnp.where(
        lax.broadcasted_iota(jnp.int32, (sd, fd), 1) // SEG
        == lax.broadcasted_iota(jnp.int32, (sd, fd), 0),
        1.0 / SEG, 0.0,
    ).astype(BF16)
    for u in range(utts):
        tail = kf.shape[1] - (LC + fd + RB)
        kf[u, pl.ds(LC + fd + RB, tail), :] = jnp.zeros((tail, half), BF16)
        vf[u, pl.ds(LC + fd + RB, tail), :] = jnp.zeros((tail, half), BF16)

    c_wf.wait()
    c_fb.wait()
    a_wf.wait_recv()
    c_mem.wait()
    a_mem.wait_recv()
    c_q.wait()
    c_k.wait()
    c_v.wait()

    def front(count, g):
        total = None
        for j in range(STACK):
            x = fb32[pl.ds(j, count, stride=STACK), :][:, :ch].astype(BF16)
            term = dot(x, wf[g, pl.ds(j * ch, ch), :])
            total = term if total is None else total + term
        return total

    def stage_a(u, carry):
        length = lengths[u]
        fb32[:, :ch] = fbv[u].astype(F32)
        ok = first + lax.broadcasted_iota(jnp.int32, (fd, half), 0) < length
        for g in range(2):
            inp[u, :, pl.ds(g * half, half)] = jnp.where(ok, front(fd, g), 0.0).astype(BF16)
        gain = gain_a[...]
        summary = dot(avg, inp[u])
        for r in range(0, sd, CH):
            nrm[pl.ds(r, CH), :] = normed_rows(summary[r : r + CH], gain)
        for r in range(0, fd, CH):
            nrm[pl.ds(sd + r, CH), :] = normed_rows(inp[u, pl.ds(r, CH), :].astype(F32), gain)
        for r in range(0, sd, CH):
            x = jnp.concatenate([mem[g, u, pl.ds(r, CH), :] for g in range(2)], axis=1)
            nrm[pl.ds(sd + fd + r, CH), :] = normed_rows(x.astype(F32), gain)
        q = dot(nrm[pl.ds(0, sd + fd), :], wq[...]).astype(BF16)
        for t in range(tiles):
            qt[u, t, pl.ds(0, TQ), :] = q[sd + t * TQ : sd + (t + 1) * TQ]
            qt[u, t, pl.ds(TQ, TS), :] = q[t * TS : (t + 1) * TS]
        for w, frame, mb in ((wk, kf, kb), (wv, vf, vb)):
            y = dot(nrm[pl.ds(sd, fd + sd), :], w[...]).astype(BF16)
            frame[u, pl.ds(LC, fd), :] = y[:fd]
            mb[u, pl.ds(M, sd), :] = y[fd:]
        return carry

    lax.fori_loop(0, utts, stage_a, 0)

    r_memh.wait_recv()
    r_fwd.start()
    r_fbl.wait_recv()
    r_fbr.wait_recv()
    nl = utts * LC
    nr = utts * RB
    for u in range(utts):
        fb32[pl.ds(u * STACK * LC, STACK * LC), :ch] = fbl[u].astype(F32)
        base = STACK * nl + u * STACK * RB
        fb32[pl.ds(base, STACK * RB), :] = jnp.zeros((STACK * RB, fb32.shape[1]), F32)
        fb32[pl.ds(base, STACK * RC), :ch] = fbr[u].astype(F32)
    row = lax.broadcasted_iota(jnp.int32, (nl + nr, half), 0)
    right = row >= nl
    which = jnp.where(right, (row - nl) // RB, row // LC)
    pos = jnp.where(right, first + fd + (row - nl) % RB, first - LC + row % LC)
    limit = jnp.full(row.shape, lengths[0], jnp.int32)
    for u in range(1, utts):
        limit = jnp.where(which == u, lengths[u], limit)
    halo = [
        jnp.where(pos < limit, front(nl + nr, g), 0.0).astype(BF16) for g in range(2)
    ]
    gain = gain_a[...]
    for r in range(0, nl + nr, CH):
        x = jnp.concatenate([h[r : r + CH] for h in halo], axis=1)
        nrm[pl.ds(r, CH), :] = normed_rows(x.astype(F32), gain)
    a_fwd.wait_recv()
    for u in range(utts):
        x = jnp.concatenate([memh[g, u] for g in range(2)], axis=1)
        nrm[pl.ds(nl + nr + u * M, M), :] = normed_rows(x.astype(F32), gain)
    for w, frame, mb in ((wk, kf, kb), (wv, vf, vb)):
        y = dot(nrm[pl.ds(0, nl + nr + utts * M), :], w[...]).astype(BF16)
        for u in range(utts):
            frame[u, pl.ds(0, LC), :] = y[u * LC : (u + 1) * LC]
            frame[u, pl.ds(LC + fd, RB), :] = y[nl + u * RB : nl + (u + 1) * RB]
            mb[u, pl.ds(0, M), :] = y[nl + nr + u * M : nl + nr + (u + 1) * M]

    for c in c_o:
        c.wait()

    def p_copy(u):
        return remote(u, part.at[u], precv.at[u], partner_id, psend, prsem)

    def m_copy(u):
        return remote(u, sums.at[u, other], srecv.at[u], partner_id, msend, mrsem)

    def f_copy(u):
        return remote(u, feed.at[u, other], frecv.at[u], partner_id, fsend, frsem)

    lane_low = lax.broadcasted_iota(jnp.int32, (TR, 2 * HEAD_DIM), 1) < HEAD_DIM
    factor = HEAD_DIM ** (-0.5) * math.log2(math.e)

    def stage_b(u, carry):
        length = lengths[u]
        for t in range(tiles):
            shape = (TR, KF + KB)
            r = lax.broadcasted_iota(jnp.int32, shape, 0)
            c = lax.broadcasted_iota(jnp.int32, shape, 1)
            seg = t * TS + jnp.where(r < TQ, r // SEG, r - TQ)
            pos = t * TQ - LC + c
            frame_ok = (
                (pos >= seg * SEG - LC) & (pos < (seg + 1) * SEG + RC)
                & (pos + first >= 0) & (pos + first < length)
            )
            rs = lax.broadcasted_iota(jnp.int32, (TR, sd), 0)
            seg_s = t * TS + jnp.where(rs < TQ, rs // SEG, rs - TQ)
            hit = lax.broadcasted_iota(jnp.int32, (TR, sd), 1) == seg_s
            low = jnp.sum(
                jnp.where(hit, (bank[pl.ds(u, 1), :] - seg0).astype(F32), 0.0),
                axis=1, keepdims=True,
            )
            j = t * TS - M + (c - KF)
            bank_ok = (j.astype(F32) >= low) & (j <= seg - 1)
            ok = ((c < KF) & frame_ok) | ((c >= KF) & bank_ok)
            bias[...] = jnp.where(ok, 0.0, NEG)
            for hp in range(half // (2 * HEAD_DIM)):
                cols = pl.ds(hp * 2 * HEAD_DIM, 2 * HEAD_DIM)
                q2 = qt[u, t, :, cols]
                k2 = jnp.concatenate(
                    [kf[u, pl.ds(t * TQ, KF), cols], kb[u, pl.ds(t * TS, KB), cols]], axis=0
                )
                v2 = jnp.concatenate(
                    [vf[u, pl.ds(t * TQ, KF), cols], vb[u, pl.ds(t * TS, KB), cols]], axis=0
                )
                outs = []
                for h in range(2):
                    keep = lane_low if h == 0 else jnp.logical_not(lane_low)
                    qm = jnp.where(keep, q2, jnp.zeros_like(q2))
                    s = lax.dot_general(
                        qm, k2, (((1,), (1,)), ((), ())), preferred_element_type=F32
                    )
                    p = jnp.exp2(s * factor + bias[...])
                    share = 1.0 / jnp.sum(p, axis=1, keepdims=True)
                    outs.append(dot((p * share).astype(BF16), v2))
                ctx[pl.ds(t * TR, TR), cols] = jnp.where(lane_low, outs[0], outs[1]).astype(BF16)
        for g in range(2):
            y = dot(ctx[...], wo[g]).astype(BF16)
            for t in range(tiles):
                part[u, g, pl.ds(t * TQ, TQ), :] = y[t * TR : t * TR + TQ]
                sums[u, g, pl.ds(t * TS, TS), :] = y[t * TR + TQ : (t + 1) * TR]
        p_copy(u).start()
        m_copy(u).start()
        return carry

    lax.fori_loop(0, utts, stage_b, 0)

    c_u.wait()
    for c in c_d:
        c.wait()

    def finish(u):
        f_copy(u).wait_recv()
        ok = first + lax.broadcasted_iota(jnp.int32, (fd, half), 0) < lengths[u]
        total = feed[u, mp].astype(F32) + frecv[u].astype(F32)
        total = hid[u, mp].astype(F32) + total
        outb[u] = jnp.where(ok, total, 0.0).astype(BF16)
        pltpu.make_async_copy(outb.at[u], enc_h.at[u], osem.at[u]).start()

    def stage_c(u, carry):
        p_copy(u).wait_recv()
        gain = gain_f[...]
        for r in range(0, fd, CH):
            xs = []
            for g in range(2):
                rows = pl.ds(r, CH)
                att = part[u, g, rows, :].astype(F32) + precv[u, g, rows, :].astype(F32)
                x = (inp[u, rows, pl.ds(g * half, half)].astype(F32) + att).astype(BF16)
                hid[u, g, rows, :] = x
                xs.append(x.astype(F32))
            nrm[pl.ds(r, CH), :] = normed_rows(jnp.concatenate(xs, axis=1), gain)
        step = 512
        for k in range(0, ff, step):
            up = dot(nrm[pl.ds(0, fd), :], wu[:, pl.ds(k, step)])
            act[:, pl.ds(k, step)] = gelu(up).astype(BF16)
        feed[u, other] = dot(act[...], wd[other]).astype(BF16)
        f_copy(u).start()
        feed[u, mp] = dot(act[...], wd[mp]).astype(BF16)

        m_copy(u).wait_recv()
        seg_ok = (seg0 + lax.broadcasted_iota(jnp.int32, (sd, half), 0)) * SEG < lengths[u]
        both = sums[u, mp].astype(F32) + srecv[u].astype(F32)
        moutb[u] = jnp.where(seg_ok, both, 0.0).astype(BF16)
        pltpu.make_async_copy(moutb.at[u], mo_h.at[u], osem.at[utts + u]).start()

        @pl.when(u > 0)
        def _():
            finish(u - 1)

        return carry

    lax.fori_loop(0, utts, stage_c, 0)
    finish(utts - 1)

    for r in (r_wf, r_mem, r_fbl, r_memh, r_fbr, r_fwd):
        r.wait_send()

    def drain(u, carry):
        p_copy(u).wait_send()
        m_copy(u).wait_send()
        f_copy(u).wait_send()
        pltpu.make_async_copy(outb.at[u], enc_h.at[u], osem.at[u]).wait()
        pltpu.make_async_copy(moutb.at[u], mo_h.at[u], osem.at[utts + u]).wait()
        return carry

    lax.fori_loop(0, utts, drain, 0)


def body(n_tm, filterbank, lengths, bank_begin, memory_in, w_front, gain_attn, w_query, w_key,
         w_value, w_out, gain_ffn, w_up, w_down):
    utts, raw, ch = filterbank.shape
    fd = raw // STACK
    sd = fd // SEG
    half = w_query.shape[1]
    full = w_query.shape[0]
    ff = w_up.shape[1]
    tiles = fd // TQ
    kf_rows = (tiles - 1) * TQ + KF
    any_spec = pl.BlockSpec(memory_space=pl.ANY)
    vmem_spec = pl.BlockSpec(memory_space=pltpu.VMEM)
    smem_spec = pl.BlockSpec(memory_space=pltpu.SMEM)
    dma = pltpu.SemaphoreType.DMA
    vm = pltpu.VMEM
    scratch = [
        vm((utts, raw, ch), BF16),
        vm((raw, 128), F32),
        vm((utts, STACK * LC, ch), BF16),
        vm((utts, STACK * RC, ch), BF16),
        vm((2,) + w_front.shape, BF16),
        vm((2, utts, sd, half), BF16),
        vm((2, utts, M, half), BF16),
        vm((full, half), BF16),
        vm((full, half), BF16),
        vm((full, half), BF16),
        vm((2, half, half), BF16),
        vm((full, ff), BF16),
        vm((2, ff, half), BF16),
        vm((utts, fd, full), BF16),
        vm((fd + 2 * sd, full), BF16),
        vm((utts, tiles, TR, half), BF16),
        vm((utts, kf_rows, half), BF16),
        vm((utts, kf_rows, half), BF16),
        vm((utts, M + sd, half), BF16),
        vm((utts, M + sd, half), BF16),
        vm((TR, KF + KB), F32),
        vm((fd + sd, half), BF16),
        vm((utts, 2, fd, half), BF16),
        vm((utts, 2, fd, half), BF16),
        vm((utts, 2, sd, half), BF16),
        vm((utts, sd, half), BF16),
        vm((utts, 2, fd, half), BF16),
        vm((fd, ff), BF16),
        vm((utts, 2, fd, half), BF16),
        vm((utts, fd, half), BF16),
        vm((utts, fd, half), BF16),
        vm((utts, sd, half), BF16),
        dma((11,)), dma((2 * utts,)), dma((6,)), dma((6,)),
        dma((utts,)), dma((utts,)), dma((utts,)), dma((utts,)), dma((utts,)), dma((utts,)),
    ]
    return pl.pallas_call(
        functools.partial(kernel, n_tm),
        out_shape=(
            jax.ShapeDtypeStruct((utts, fd, half), BF16),
            jax.ShapeDtypeStruct((utts, sd, half), BF16),
        ),
        in_specs=[smem_spec, vmem_spec, vmem_spec, vmem_spec] + [any_spec] * 9,
        out_specs=(any_spec, any_spec),
        scratch_shapes=scratch,
        compiler_params=pltpu.CompilerParams(
            collective_id=0, has_side_effects=True, vmem_limit_bytes=60 * 1024 * 1024
        ),
    )(
        lengths, bank_begin, gain_attn.reshape(1, full), gain_ffn.reshape(1, full),
        filterbank, memory_in, w_front, w_query, w_key, w_value, w_out, w_up, w_down,
    )


def solution(mesh):
    in_specs = (
        P(None, "tm", None),
        P(),
        P(None, "tm"),
        P(None, "tm", "mp"),
        P(None, "mp"),
        P(),
        P(None, "mp"),
        P(None, "mp"),
        P(None, "mp"),
        P("mp", None),
        P(),
        P(None, "mp"),
        P("mp", None),
    )
    out_specs = (P(None, "tm", "mp"), P(None, "tm", "mp"))
    return jax.shard_map(
        functools.partial(body, mesh.shape["tm"]),
        mesh=mesh, in_specs=in_specs, out_specs=out_specs, check_vma=False,
    )
```

time: 167 us -> 49.4 us (0.30)
  matrix products: 48.1 us -> 0 us
  Pallas kernels: 0 us -> 42.4 us
  waiting for transfers between devices: 37.4 us -> 0 us
  other arithmetic: 23.9 us -> 0 us
  local copies, waits for them, and re-layouts: 26 us -> 6.13 us
  between operations: 14.3 us -> 0.64 us
  starting transfers between devices: 11.5 us -> 0 us
  blocking collectives: 4.79 us -> 0 us
    dot_general x8 -> x0, matrix products: 48.1 us -> none  [the longest x6 24.3 us: product(): result = jnp.dot(flat_rows, weight, preferred_element_type=jnp.float32)]
    pallas_call x0 -> x1, Pallas kernels: none -> 42.4 us  [body(): pl.pallas_call(functools.partial(kernel, n_tm), out_shape=(jax.ShapeDtype...]
    reduce_scatter x3 -> x0, waiting for transfers between devices: 19 us -> none  [the longest x1 9.89 us: body(): lax.psum_scatter(frame_term.astype(jnp.bfloat16), 'mp', scatter_dimension...]
    all_gather x2 -> x0, waiting for transfers between devices: 18.3 us -> none  [the longest x1 9.98 us: body(): normed_ffn = lax.all_gather(normed_half, 'mp', axis=2, tiled=True)]
    reduce_sum x8 -> x0, other arithmetic: 12.1 us -> none  [the longest x1 5.92 us: body(): jnp.mean(inputs_f.reshape(batch_count, segs_dev, SEG, full_width), axis=2)]
    ppermute x3 -> x0, starting transfers between devices: 11.1 us -> none  [from_behind(): return lax.ppermute(block, axis, route)]
    slice x13 -> x0, local copies, waits for them, and re-layouts: 9.59 us -> none  [the longest x3 2.52 us: body(): frame_keys = key_rows[:, :frames_dev]]
    convert_element_type x3 -> x0, other arithmetic: 5.7 us -> none  [the longest x1 2.54 us: body(): encoded = jnp.where(valid_frame[:, :, None], residual.astype(jnp.float32)...]
  transfers between devices with their start and end apart: 8 -> 0, of which waited for: 4 -> 0; matrix products, arithmetic and copies ran while one was open for 21% -> 0% of each run, Pallas kernels for 0% -> 0%
where the time goes in v1:
time: 49.4 us; the launch traced here: 49.1 us
  Pallas kernels  42.4 us (86%)
  local copies, waits for them, and re-layouts  6.13 us (12%)
  between operations  0.64 us (1%)
    pallas_call x1, Pallas kernels, body(): pl.pallas_call(functools.partial(kernel, n_tm), out_shape=(jax.ShapeDtype...  42.4 us
    unnamed x3, local copies, waits for them, and re-layouts  6.13 us

profile of v1, /device:TPU:0, one launch (start us, length us, event | category | flops | bytes accessed | tf_op | source)
XLA Modules:
  0.0 49.1 jit_solution(18315428510381944095)
XLA Ops:
  0.6 2.2 %copy.15.fb_h = bf16[4,1024,80]{2,1,0:T(8,128)(2,1)} copy(bf16[4,1024,80]{1,2,0:T(8,128)(2,1)} %param.13) | data formatting | bytes 1310720 | tf_op args[0]
  2.8 42.4 %shard_map.140 = (bf16[4,256,512]{2,1,0:T(8,128)(2,1)}, bf16[4,64,512]{2,1,0:T(8,128)(2,1)}) custom-call(s32[4]{0:T(128)} %lengths.1, s32[4,64]{1,0:T(4,128)} %bank.1, f32[1,1024]{1,0:T(1,128)} %bitcast.2, f32[1,1024]{1,0:T(1,128)} %bitcast.3, bf16[4,1024,80]{2,1,0:T(8,128)(2,1)} %copy.15.fb_h, bf16[4,64,512]{2,1,0:T(8,128)(2,1)} %mem_h.1, ...), custom_call_target="tpu_custom_call" | custom-call | tf_op jit(solution)/shard_map/pallas_call | solution.py:386
  45.2 2.3 %copy.18 = bf16[4,256,512]{2,1,0:T(8,128)(2,1)} copy(bf16[4,256,512]{2,1,0:T(8,128)(2,1)} %get-tuple-element.4) | data formatting | bytes 2097152
  47.5 1.7 %copy.19 = bf16[4,64,512]{2,1,0:T(8,128)(2,1)} copy(bf16[4,64,512]{2,1,0:T(8,128)(2,1)} %get-tuple-element.5) | data formatting | bytes 524288

commit v2 on v1

--- a/solution.py
+++ b/solution.py
@@ -43,20 +43,21 @@
 
 
 def gelu(v):
-    inner = math.sqrt(2.0 / math.pi) * (v + 0.044715 * (v * v * v))
-    return 0.5 * v * (1.0 + jnp.tanh(inner))
+    c = math.sqrt(2.0 / math.pi)
+    half_v = 0.5 * v
+    return half_v + half_v * jnp.tanh(v * (c + (0.044715 * c) * (v * v)))
 
 
 def kernel(
     n_tm,
     lengths, bank, gain_a, gain_f, fb_h, mem_h, wf_h, wq_h, wk_h, wv_h, wo_h, wu_h, wd_h,
-    enc_h, mo_h,
+    outb, moutb,
     fbv, fb32, fbl, fbr, wf, mem, memh, wq, wk, wv, wo, wu, wd,
-    inp, nrm, qt, kf, vf, kb, vb, bias, ctx, part, precv, sums, srecv,
-    hid, act, feed, frecv, outb, moutb,
-    lsem, osem, ssem, rsem, psend, prsem, msend, mrsem, fsend, frsem,
+    inp, nrm, stk, smry, qt, kf, vf, kb, vb, bias, ctx, part, precv, sums, srecv,
+    hid, act, feed, frecv,
+    lsem, ssem, rsem, psend, prsem, msend, mrsem, fsend, frsem,
 ):
-    utts, raw, ch = fb_h.shape
+    utts, ch, raw = fb_h.shape
     fd = raw // STACK
     sd = fd // SEG
     half = mem_h.shape[2]
@@ -102,9 +103,9 @@
     pl.semaphore_wait(barrier, 3)
     r_wf = remote(0, wf_h, wf.at[mp], partner_id)
     r_mem = remote(1, mem_h, mem.at[mp], partner_id)
-    r_fbl = remote(2, fb_h.at[:, pl.ds(raw - STACK * LC, STACK * LC), :], fbl, next_id)
+    r_fbl = remote(2, fb_h.at[:, :, pl.ds(raw - STACK * LC, STACK * LC)], fbl, next_id)
     r_memh = remote(3, mem_h.at[:, pl.ds(sd - M, M), :], memh.at[mp], next_id)
-    r_fbr = remote(4, fb_h.at[:, pl.ds(0, STACK * RC), :], fbr, prev_id)
+    r_fbr = remote(4, fb_h.at[:, :, pl.ds(0, STACK * LC)], fbr, prev_id)
     r_fwd = remote(5, memh.at[mp], memh.at[mp], partner_id)
     for r in (r_wf, r_mem, r_fbl, r_memh, r_fbr):
         r.start()
@@ -131,37 +132,99 @@
     c_k.wait()
     c_v.wait()
 
-    def front(count, g):
-        total = None
-        for j in range(STACK):
-            x = fb32[pl.ds(j, count, stride=STACK), :][:, :ch].astype(BF16)
-            term = dot(x, wf[g, pl.ds(j * ch, ch), :])
-            total = term if total is None else total + term
-        return total
+    def stacked(count):
+        parts = [fb32[pl.ds(j, count, stride=STACK), :][:, :ch] for j in range(STACK)]
+        return jnp.concatenate(parts, axis=1).astype(BF16)
+
+    factor = HEAD_DIM ** (-0.5) * math.log2(math.e)
+
+    def front(u):
+        fb32[:, :ch] = fbv[u].astype(F32).T
+        stk[...] = stacked(fd)
+        ok = first + lax.broadcasted_iota(jnp.int32, (fd, half), 0) < lengths[u]
+        for g in range(2):
+            inp[u, :, pl.ds(g * half, half)] = jnp.where(ok, dot(stk[...], wf[g]), 0.0).astype(BF16)
+        smry[...] = dot(avg, inp[u])
+
+    def norm_tasks(u):
+        dst = nrm
+        gain = gain_a[...]
+
+        def of_summary(r):
+            dst[pl.ds(r, CH), :] = normed_rows(smry[pl.ds(r, CH), :], gain)
+
+        def of_frames(r):
+            dst[pl.ds(sd + r, CH), :] = normed_rows(inp[u, pl.ds(r, CH), :].astype(F32), gain)
+
+        def of_memory(r):
+            x = jnp.concatenate([mem[g, u, pl.ds(r, CH), :] for g in range(2)], axis=1)
+            dst[pl.ds(sd + fd + r, CH), :] = normed_rows(x.astype(F32), gain)
+
+        return (
+            [functools.partial(of_summary, r) for r in range(0, sd, CH)]
+            + [functools.partial(of_frames, r) for r in range(0, fd, CH)]
+            + [functools.partial(of_memory, r) for r in range(0, sd, CH)]
+        )
+
+    def make_bias(u, t):
+        length = lengths[u]
+        shape = (TR, KF + KB)
+        r = lax.broadcasted_iota(jnp.int32, shape, 0)
+        c = lax.broadcasted_iota(jnp.int32, shape, 1)
+        seg = t * TS + jnp.where(r < TQ, r // SEG, r - TQ)
+        pos = t * TQ - LC + c
+        frame_ok = (
+            (pos >= seg * SEG - LC) & (pos < (seg + 1) * SEG + RC)
+            & (pos + first >= 0) & (pos + first < length)
+        )
+        rs = lax.broadcasted_iota(jnp.int32, (TR, sd), 0)
+        seg_s = t * TS + jnp.where(rs < TQ, rs // SEG, rs - TQ)
+        hit = lax.broadcasted_iota(jnp.int32, (TR, sd), 1) == seg_s
+        low = jnp.sum(
+            jnp.where(hit, (bank[pl.ds(u, 1), :] - seg0).astype(F32), 0.0),
+            axis=1, keepdims=True,
+        )
+        j = t * TS - M + (c - KF)
+        bank_ok = (j.astype(F32) >= low) & (j <= seg - 1)
+        ok = ((c < KF) & frame_ok) | ((c >= KF) & bank_ok)
+        bias[u, t] = jnp.where(ok, 0.0, NEG)
+
+    def spread_over(tasks, pieces):
+        done = 0
+        for i, piece in enumerate(pieces):
+            upto = len(tasks) * (i + 1) // len(pieces)
+            for task in tasks[done:upto]:
+                task()
+            done = upto
+            piece()
+
+    def qkv_pieces(u):
+        src = nrm
+        wide = half // 2
+
+        def query(n):
+            q = dot(src[pl.ds(0, sd + fd), :], wq[:, pl.ds(n, wide)]).astype(BF16)
+            for t in range(tiles):
+                qt[u, t, pl.ds(0, TQ), pl.ds(n, wide)] = q[sd + t * TQ : sd + (t + 1) * TQ]
+                qt[u, t, pl.ds(TQ, TS), pl.ds(n, wide)] = q[t * TS : (t + 1) * TS]
+
+        def key_value(w, frame, mb, n):
+            y = dot(src[pl.ds(sd, fd + sd), :], w[:, pl.ds(n, wide)]).astype(BF16)
+            frame[u, pl.ds(LC, fd), pl.ds(n, wide)] = y[:fd]
+            mb[u, pl.ds(M, sd), pl.ds(n, wide)] = y[fd:]
+
+        cuts = range(0, half, wide)
+        return (
+            [functools.partial(query, n) for n in cuts]
+            + [functools.partial(key_value, wk, kf, kb, n) for n in cuts]
+            + [functools.partial(key_value, wv, vf, vb, n) for n in cuts]
+        )
 
     def stage_a(u, carry):
-        length = lengths[u]
-        fb32[:, :ch] = fbv[u].astype(F32)
-        ok = first + lax.broadcasted_iota(jnp.int32, (fd, half), 0) < length
-        for g in range(2):
-            inp[u, :, pl.ds(g * half, half)] = jnp.where(ok, front(fd, g), 0.0).astype(BF16)
-        gain = gain_a[...]
-        summary = dot(avg, inp[u])
-        for r in range(0, sd, CH):
-            nrm[pl.ds(r, CH), :] = normed_rows(summary[r : r + CH], gain)
-        for r in range(0, fd, CH):
-            nrm[pl.ds(sd + r, CH), :] = normed_rows(inp[u, pl.ds(r, CH), :].astype(F32), gain)
-        for r in range(0, sd, CH):
-            x = jnp.concatenate([mem[g, u, pl.ds(r, CH), :] for g in range(2)], axis=1)
-            nrm[pl.ds(sd + fd + r, CH), :] = normed_rows(x.astype(F32), gain)
-        q = dot(nrm[pl.ds(0, sd + fd), :], wq[...]).astype(BF16)
-        for t in range(tiles):
-            qt[u, t, pl.ds(0, TQ), :] = q[sd + t * TQ : sd + (t + 1) * TQ]
-            qt[u, t, pl.ds(TQ, TS), :] = q[t * TS : (t + 1) * TS]
-        for w, frame, mb in ((wk, kf, kb), (wv, vf, vb)):
-            y = dot(nrm[pl.ds(sd, fd + sd), :], w[...]).astype(BF16)
-            frame[u, pl.ds(LC, fd), :] = y[:fd]
-            mb[u, pl.ds(M, sd), :] = y[fd:]
+        front(u)
+        for task in norm_tasks(u):
+            task()
+        spread_over([functools.partial(make_bias, u, t) for t in range(tiles)], qkv_pieces(u))
         return carry
 
     lax.fori_loop(0, utts, stage_a, 0)
@@ -173,10 +236,9 @@
     nl = utts * LC
     nr = utts * RB
     for u in range(utts):
-        fb32[pl.ds(u * STACK * LC, STACK * LC), :ch] = fbl[u].astype(F32)
+        fb32[pl.ds(u * STACK * LC, STACK * LC), :ch] = fbl[u].astype(F32).T
         base = STACK * nl + u * STACK * RB
-        fb32[pl.ds(base, STACK * RB), :] = jnp.zeros((STACK * RB, fb32.shape[1]), F32)
-        fb32[pl.ds(base, STACK * RC), :ch] = fbr[u].astype(F32)
+        fb32[pl.ds(base, STACK * RB), :ch] = fbr[u].astype(F32).T[: STACK * RB]
     row = lax.broadcasted_iota(jnp.int32, (nl + nr, half), 0)
     right = row >= nl
     which = jnp.where(right, (row - nl) // RB, row // LC)
@@ -184,8 +246,10 @@
     limit = jnp.full(row.shape, lengths[0], jnp.int32)
     for u in range(1, utts):
         limit = jnp.where(which == u, lengths[u], limit)
+    stk[pl.ds(0, nl + nr), :] = stacked(nl + nr)
     halo = [
-        jnp.where(pos < limit, front(nl + nr, g), 0.0).astype(BF16) for g in range(2)
+        jnp.where(pos < limit, dot(stk[pl.ds(0, nl + nr), :], wf[g]), 0.0).astype(BF16)
+        for g in range(2)
     ]
     gain = gain_a[...]
     for r in range(0, nl + nr, CH):
@@ -215,31 +279,8 @@
         return remote(u, feed.at[u, other], frecv.at[u], partner_id, fsend, frsem)
 
     lane_low = lax.broadcasted_iota(jnp.int32, (TR, 2 * HEAD_DIM), 1) < HEAD_DIM
-    factor = HEAD_DIM ** (-0.5) * math.log2(math.e)
-
     def stage_b(u, carry):
-        length = lengths[u]
         for t in range(tiles):
-            shape = (TR, KF + KB)
-            r = lax.broadcasted_iota(jnp.int32, shape, 0)
-            c = lax.broadcasted_iota(jnp.int32, shape, 1)
-            seg = t * TS + jnp.where(r < TQ, r // SEG, r - TQ)
-            pos = t * TQ - LC + c
-            frame_ok = (
-                (pos >= seg * SEG - LC) & (pos < (seg + 1) * SEG + RC)
-                & (pos + first >= 0) & (pos + first < length)
-            )
-            rs = lax.broadcasted_iota(jnp.int32, (TR, sd), 0)
-            seg_s = t * TS + jnp.where(rs < TQ, rs // SEG, rs - TQ)
-            hit = lax.broadcasted_iota(jnp.int32, (TR, sd), 1) == seg_s
-            low = jnp.sum(
-                jnp.where(hit, (bank[pl.ds(u, 1), :] - seg0).astype(F32), 0.0),
-                axis=1, keepdims=True,
-            )
-            j = t * TS - M + (c - KF)
-            bank_ok = (j.astype(F32) >= low) & (j <= seg - 1)
-            ok = ((c < KF) & frame_ok) | ((c >= KF) & bank_ok)
-            bias[...] = jnp.where(ok, 0.0, NEG)
             for hp in range(half // (2 * HEAD_DIM)):
                 cols = pl.ds(hp * 2 * HEAD_DIM, 2 * HEAD_DIM)
                 q2 = qt[u, t, :, cols]
@@ -256,7 +297,7 @@
                     s = lax.dot_general(
                         qm, k2, (((1,), (1,)), ((), ())), preferred_element_type=F32
                     )
-                    p = jnp.exp2(s * factor + bias[...])
+                    p = jnp.exp2(s * factor + bias[u, t])
                     share = 1.0 / jnp.sum(p, axis=1, keepdims=True)
                     outs.append(dot((p * share).astype(BF16), v2))
                 ctx[pl.ds(t * TR, TR), cols] = jnp.where(lane_low, outs[0], outs[1]).astype(BF16)
@@ -275,39 +316,55 @@
     for c in c_d:
         c.wait()
 
-    def finish(u):
-        f_copy(u).wait_recv()
-        ok = first + lax.broadcasted_iota(jnp.int32, (fd, half), 0) < lengths[u]
-        total = feed[u, mp].astype(F32) + frecv[u].astype(F32)
-        total = hid[u, mp].astype(F32) + total
-        outb[u] = jnp.where(ok, total, 0.0).astype(BF16)
-        pltpu.make_async_copy(outb.at[u], enc_h.at[u], osem.at[u]).start()
-
-    def stage_c(u, carry):
-        p_copy(u).wait_recv()
-        gain = gain_f[...]
-        for r in range(0, fd, CH):
-            xs = []
-            for g in range(2):
-                rows = pl.ds(r, CH)
-                att = part[u, g, rows, :].astype(F32) + precv[u, g, rows, :].astype(F32)
-                x = (inp[u, rows, pl.ds(g * half, half)].astype(F32) + att).astype(BF16)
-                hid[u, g, rows, :] = x
-                xs.append(x.astype(F32))
-            nrm[pl.ds(r, CH), :] = normed_rows(jnp.concatenate(xs, axis=1), gain)
-        step = 512
-        for k in range(0, ff, step):
-            up = dot(nrm[pl.ds(0, fd), :], wu[:, pl.ds(k, step)])
-            act[:, pl.ds(k, step)] = gelu(up).astype(BF16)
-        feed[u, other] = dot(act[...], wd[other]).astype(BF16)
-        f_copy(u).start()
-        feed[u, mp] = dot(act[...], wd[mp]).astype(BF16)
-
-        m_copy(u).wait_recv()
+    def finish_tasks(u):
+        def part_of(r):
+            rows = pl.ds(r, CH)
+            ok = first + r + lax.broadcasted_iota(jnp.int32, (CH, half), 0) < lengths[u]
+            total = hid[u, mp, rows, :] + (feed[u, mp, rows, :] + frecv[u, rows, :])
+            outb[u, rows, :] = jnp.where(ok, total, jnp.zeros_like(total))
+
+        return [functools.partial(part_of, r) for r in range(0, fd, CH)]
+
+    def summary_out(u):
         seg_ok = (seg0 + lax.broadcasted_iota(jnp.int32, (sd, half), 0)) * SEG < lengths[u]
         both = sums[u, mp].astype(F32) + srecv[u].astype(F32)
         moutb[u] = jnp.where(seg_ok, both, 0.0).astype(BF16)
-        pltpu.make_async_copy(moutb.at[u], mo_h.at[u], osem.at[utts + u]).start()
+
+    def hidden_tasks(u):
+        dst = nrm
+        gain = gain_f[...]
+
+        def part_of(r):
+            xs = []
+            rows = pl.ds(r, CH)
+            for g in range(2):
+                att = part[u, g, rows, :] + precv[u, g, rows, :]
+                x = inp[u, rows, pl.ds(g * half, half)] + att
+                hid[u, g, rows, :] = x
+                xs.append(x.astype(F32))
+            dst[rows, :] = normed_rows(jnp.concatenate(xs, axis=1), gain)
+
+        return [functools.partial(part_of, r) for r in range(0, fd, CH)]
+
+    step = 512
+
+    def finish(u):
+        f_copy(u).wait_recv()
+        for task in finish_tasks(u):
+            task()
+
+    def stage_c(u, carry):
+        p_copy(u).wait_recv()
+        for task in hidden_tasks(u):
+            task()
+        for k in range(0, ff, step):
+            up = dot(nrm[pl.ds(0, fd), :], wu[:, pl.ds(k, step)])
+            act[:, pl.ds(k, step)] = gelu(up.astype(BF16))
+        feed[u, other] = dot(act[...], wd[other]).astype(BF16)
+        f_copy(u).start()
+        m_copy(u).wait_recv()
+        summary_out(u)
+        feed[u, mp] = dot(act[...], wd[mp]).astype(BF16)
 
         @pl.when(u > 0)
         def _():
@@ -325,8 +382,6 @@
         p_copy(u).wait_send()
         m_copy(u).wait_send()
         f_copy(u).wait_send()
-        pltpu.make_async_copy(outb.at[u], enc_h.at[u], osem.at[u]).wait()
-        pltpu.make_async_copy(moutb.at[u], mo_h.at[u], osem.at[utts + u]).wait()
         return carry
 
     lax.fori_loop(0, utts, drain, 0)
@@ -348,10 +403,10 @@
     dma = pltpu.SemaphoreType.DMA
     vm = pltpu.VMEM
     scratch = [
-        vm((utts, raw, ch), BF16),
+        vm((utts, ch, raw), BF16),
         vm((raw, 128), F32),
-        vm((utts, STACK * LC, ch), BF16),
-        vm((utts, STACK * RC, ch), BF16),
+        vm((utts, ch, STACK * LC), BF16),
+        vm((utts, ch, STACK * LC), BF16),
         vm((2,) + w_front.shape, BF16),
         vm((2, utts, sd, half), BF16),
         vm((2, utts, M, half), BF16),
@@ -363,12 +418,14 @@
         vm((2, ff, half), BF16),
         vm((utts, fd, full), BF16),
         vm((fd + 2 * sd, full), BF16),
+        vm((fd, STACK * ch), BF16),
+        vm((sd, full), F32),
         vm((utts, tiles, TR, half), BF16),
         vm((utts, kf_rows, half), BF16),
         vm((utts, kf_rows, half), BF16),
         vm((utts, M + sd, half), BF16),
         vm((utts, M + sd, half), BF16),
-        vm((TR, KF + KB), F32),
+        vm((utts, tiles, TR, KF + KB), F32),
         vm((fd + sd, half), BF16),
         vm((utts, 2, fd, half), BF16),
         vm((utts, 2, fd, half), BF16),
@@ -378,26 +435,24 @@
         vm((fd, ff), BF16),
         vm((utts, 2, fd, half), BF16),
         vm((utts, fd, half), BF16),
-        vm((utts, fd, half), BF16),
-        vm((utts, sd, half), BF16),
-        dma((11,)), dma((2 * utts,)), dma((6,)), dma((6,)),
+        dma((11,)), dma((6,)), dma((6,)),
         dma((utts,)), dma((utts,)), dma((utts,)), dma((utts,)), dma((utts,)), dma((utts,)),
     ]
     return pl.pallas_call(
         functools.partial(kernel, n_tm),
         out_shape=(
-            jax.ShapeDtypeStruct((utts, fd, half), BF16),
-            jax.ShapeDtypeStruct((utts, sd, half), BF16),
+            pltpu.VMEM((utts, fd, half), BF16),
+            pltpu.VMEM((utts, sd, half), BF16),
         ),
         in_specs=[smem_spec, vmem_spec, vmem_spec, vmem_spec] + [any_spec] * 9,
-        out_specs=(any_spec, any_spec),
+        out_specs=(vmem_spec, vmem_spec),
         scratch_shapes=scratch,
         compiler_params=pltpu.CompilerParams(
             collective_id=0, has_side_effects=True, vmem_limit_bytes=60 * 1024 * 1024
         ),
     )(
         lengths, bank_begin, gain_attn.reshape(1, full), gain_ffn.reshape(1, full),
-        filterbank, memory_in, w_front, w_query, w_key, w_value, w_out, w_up, w_down,
+        jnp.swapaxes(filterbank, 1, 2), memory_in, w_front, w_query, w_key, w_value, w_out, w_up, w_down,
     )
 
 

time: 49.4 us -> 42.2 us (0.85)
  local copies, waits for them, and re-layouts: 6.13 us -> 1.67 us
  Pallas kernels: 42.4 us -> 39.7 us
    unnamed x3 -> x2, local copies, waits for them, and re-layouts: 6.13 us -> 1.67 us
    pallas_call x1, Pallas kernels: 42.4 us -> 39.7 us  [body(): pl.pallas_call(functools.partial(kernel, n_tm), out_shape=(pltpu.VMEM((ut...]
where the time goes in v2:
time: 42.2 us; the launch traced here: 42.1 us
  Pallas kernels  39.7 us (94%)
  local copies, waits for them, and re-layouts  1.67 us (4%)
  between operations  0.64 us (2%)
    pallas_call x1, Pallas kernels, body(): pl.pallas_call(functools.partial(kernel, n_tm), out_shape=(pltpu.VMEM((ut...  39.7 us
    unnamed x2, local copies, waits for them, and re-layouts  1.67 us

profile of v2, /device:TPU:0, one launch (start us, length us, event | category | flops | bytes accessed | tf_op | source)
XLA Modules:
  0.0 42.1 jit_solution(4585374712819632249)
XLA Ops:
  0.6 39.7 %shard_map.140 = (bf16[4,256,512]{2,1,0:T(8,128)(2,1)S(1)}, bf16[4,64,512]{2,1,0:T(8,128)(2,1)S(1)}) custom-call(s32[4]{0:T(128)} %lengths.1, s32[4,64]{1,0:T(4,128)} %bank.1, f32[1,1024]{1,0:T(1,128)} %bitcast.4, f32[1,1024]{1,0:T(1,128)} %bitcast.5, bf16[4,80,1024]{2,1,0:T(8,128)(2,1)} %bitcast.3, bf16[4,64,512]{2,1,0:T(8,128)(2,1)} %mem_h.1, ...), custom_call_target="tpu_custom_call" | custom-call | tf_op jit(solution)/shard_map/pallas_call | solution.py:441
  40.4 1.0 %copy.17 = bf16[4,256,512]{2,1,0:T(8,128)(2,1)} copy(bf16[4,256,512]{2,1,0:T(8,128)(2,1)S(1)} %get-tuple-element.2) | data formatting | bytes 2097152
  41.4 0.7 %copy.18 = bf16[4,64,512]{2,1,0:T(8,128)(2,1)} copy(bf16[4,64,512]{2,1,0:T(8,128)(2,1)S(1)} %get-tuple-element.3) | data formatting | bytes 524288
